TPU v7x, 32 devices: a whole 2x2x4 slice. The times are simulated.
32 devices in a mesh: rep: 8 (over y, x, core), shard: 4 (over z).
Axes of the slice: x: 2, y: 2, z: 4, core: 2. Of those that a mesh axis runs over, the one named last changes fastest.
Arguments:
- tokens: bfloat16 [4096, 768], P(('rep', 'shard')), may hold values from -30 to 30
- segments: int32 [32, 128], P(('rep', 'shard')), may hold values from 0 to 7, never falling along the last dimension, each value on 1 to 64 neighbouring positions
- w_query: bfloat16 [768, 768], P('shard'), may hold values from -0.21875 to 0.21875
- w_key: bfloat16 [768, 768], P('shard'), may hold values from -0.21875 to 0.21875
- w_value: bfloat16 [768, 768], P('shard'), may hold values from -0.21875 to 0.21875
- w_out: bfloat16 [768, 768], P('shard'), may hold values from -0.875 to 0.875
- b_query: bfloat16 [768], P('shard'), may hold values from -3 to 3
- b_value: bfloat16 [768], P('shard'), may hold values from -3 to 3
- b_out: bfloat16 [768], P('shard'), may hold values from -3 to 3
- gain_one: bfloat16 [768], P('shard'), may hold values from 0.099609375 to 1.8984375
- shift_one: bfloat16 [768], P('shard'), may hold values from -3 to 3
- w_up: bfloat16 [768, 3072], P('shard'), may hold values from -0.21875 to 0.21875
- b_up: bfloat16 [3072], P('shard'), may hold values from -3 to 3
- w_down: bfloat16 [3072, 768], P('shard'), may hold values from -0.109375 to 0.109375
- b_down: bfloat16 [768], P('shard'), may hold values from -3 to 3
- gain_two: bfloat16 [768], P('shard'), may hold values from 0.099609375 to 1.8984375
- shift_two: bfloat16 [768], P('shard'), may hold values from -3 to 3
- cotangent: bfloat16 [4096, 768], P(('rep', 'shard')), may hold values from -6 to 6
Outputs:
- output: bfloat16 [4096, 768], P(('rep', 'shard'))
- grad_tokens: bfloat16 [4096, 768], P(('rep', 'shard'))
- grad_w_query: float32 [768, 768], P('shard')
- grad_w_key: float32 [768, 768], P('shard')
- grad_w_value: float32 [768, 768], P('shard')
- grad_w_out: float32 [768, 768], P('shard')
- grad_b_query: float32 [768], P('shard')
- grad_b_value: float32 [768], P('shard')
- grad_b_out: float32 [768], P('shard')
- grad_gain_one: float32 [768], P('shard')
- grad_shift_one: float32 [768], P('shard')
- grad_w_up: float32 [768, 3072], P('shard')
- grad_b_up: float32 [3072], P('shard')
- grad_w_down: float32 [3072, 768], P('shard')
- grad_b_down: float32 [768], P('shard')
- grad_gain_two: float32 [768], P('shard')
- grad_shift_two: float32 [768], P('shard')
Inputs may be any that keep to these rules, and one draw needn't show every extreme that they name: `segments`: segment numbers never fall along a row; each segment holds 1 to 64 tokens, and in every row exactly one segment holds 64 tokens.
All inputs are finite; a program needn't handle non-finite values.
Results may differ from a plain program's by a relative error of at most 0.014.
The roundings to bfloat16 on the way count: a program that leaves them out, or rounds other values in their place, can miss the bound.
Values may be sent and summed in bfloat16 or wider, within the bound.
A program may use at most 128 MiB of HBM per device.

v0:
```python
import math
import jax
import jax.numpy as jnp
from jax import lax
from jax.sharding import PartitionSpec as P

HEAD_DIM = 64
epsilon = 1e-05
masked_value = -1e30
root_half = 0.7071067811865476
inv_root_tau = 0.3989422804014327


def layer_norm(hidden, gain, shift):
    center = hidden - jnp.mean(hidden, axis=-1, keepdims=True)
    inv_std = lax.rsqrt(jnp.mean(center * center, axis=-1, keepdims=True) + epsilon)
    normed = center * inv_std
    return (normed * gain + shift, normed, inv_std)


def norm_back(upstream, normed, inv_std, gain):
    scaled = upstream * gain
    grad_in = inv_std * (
        scaled
        - jnp.mean(scaled, axis=-1, keepdims=True)
        - normed * jnp.mean(scaled * normed, axis=-1, keepdims=True)
    )
    return (grad_in, jnp.sum(upstream * normed, axis=0), jnp.sum(upstream, axis=0))


def gelu_value(pre):
    return 0.5 * pre * (1.0 + lax.erf(pre * root_half))


def gelu_slope(pre):
    return 0.5 * (1.0 + lax.erf(pre * root_half)) + pre * jnp.exp(-0.5 * pre * pre) * inv_root_tau


def masked_scores(queries, keys, seg_block, scale):
    scores = (
        jnp.einsum("gqhe,gkhe->ghqk", queries, keys, preferred_element_type=jnp.float32) * scale
    )
    allowed = (seg_block[:, :, None] == seg_block[:, None, :])[:, None]
    return jnp.where(allowed, scores, masked_value)


def dense(left, right):
    return jnp.dot(left, right, preferred_element_type=jnp.float32)


def body(
    tokens,
    segments,
    w_query,
    w_key,
    w_value,
    w_out,
    b_query,
    b_value,
    b_out,
    gain_one,
    shift_one,
    w_up,
    b_up,
    w_down,
    b_down,
    gain_two,
    shift_two,
    cotangent,
):
    f32 = jnp.float32
    bf16 = jnp.bfloat16
    fwd_set = (
        lax.all_gather(w_query, "shard", axis=0, tiled=True),
        lax.all_gather(w_key, "shard", axis=0, tiled=True),
        lax.all_gather(w_value, "shard", axis=0, tiled=True),
        lax.all_gather(w_out, "shard", axis=0, tiled=True),
        lax.all_gather(b_query, "shard", axis=0, tiled=True),
        lax.all_gather(b_value, "shard", axis=0, tiled=True),
        lax.all_gather(b_out, "shard", axis=0, tiled=True),
        lax.all_gather(gain_one, "shard", axis=0, tiled=True),
        lax.all_gather(shift_one, "shard", axis=0, tiled=True),
        lax.all_gather(w_up, "shard", axis=0, tiled=True),
        lax.all_gather(b_up, "shard", axis=0, tiled=True),
        lax.all_gather(w_down, "shard", axis=0, tiled=True),
        lax.all_gather(b_down, "shard", axis=0, tiled=True),
        lax.all_gather(gain_two, "shard", axis=0, tiled=True),
        lax.all_gather(shift_two, "shard", axis=0, tiled=True),
    )
    (
        full_query,
        full_key,
        full_value,
        full_out,
        bias_query,
        bias_value,
        bias_out,
        full_gain_one,
        full_shift_one,
        full_up,
        bias_up,
        full_down,
        bias_down,
        full_gain_two,
        full_shift_two,
    ) = fwd_set
    rows_here, seq_len = segments.shape
    width = tokens.shape[1]
    heads_count = width // HEAD_DIM
    scale = 1.0 / math.sqrt(HEAD_DIM)

    def split_heads(matrix):
        return matrix.reshape(rows_here, seq_len, heads_count, HEAD_DIM)

    queries = (dense(tokens, full_query) + bias_query.astype(f32)).astype(bf16)
    keys = dense(tokens, full_key).astype(bf16)
    values = (dense(tokens, full_value) + bias_value.astype(f32)).astype(bf16)
    q_heads, k_heads, v_heads = (split_heads(queries), split_heads(keys), split_heads(values))
    scores = masked_scores(q_heads, k_heads, segments, scale)
    top = jnp.max(scores, axis=-1, keepdims=True)
    log_total = top + jnp.log(jnp.sum(jnp.exp(scores - top), axis=-1, keepdims=True))
    probs = jnp.exp(scores - log_total).astype(bf16)
    context = (
        jnp.einsum("ghqk,gkhe->gqhe", probs, v_heads, preferred_element_type=f32)
        .astype(bf16)
        .reshape(-1, width)
    )
    resid_one = tokens.astype(f32) + dense(context, full_out) + bias_out.astype(f32)
    norm_one, normed_one, inv_one = layer_norm(
        resid_one, full_gain_one.astype(f32), full_shift_one.astype(f32)
    )
    norm_one_b = norm_one.astype(bf16)
    pre_act = dense(norm_one_b, full_up) + bias_up.astype(f32)
    act = gelu_value(pre_act).astype(bf16)
    resid_two = norm_one + dense(act, full_down) + bias_down.astype(f32)
    final, normed_two, inv_two = layer_norm(
        resid_two, full_gain_two.astype(f32), full_shift_two.astype(f32)
    )
    output = final.astype(bf16)
    back_query, back_key, back_value, back_out = (full_query, full_key, full_value, full_out)
    back_up, back_down, back_gain_one, back_gain_two = (
        full_up,
        full_down,
        full_gain_one,
        full_gain_two,
    )
    g_resid_two, g_gain_two, g_shift_two = norm_back(
        cotangent.astype(f32), normed_two, inv_two, back_gain_two.astype(f32)
    )
    g_two_b = g_resid_two.astype(bf16)
    g_b_down = jnp.sum(g_resid_two, axis=0)
    g_pre = dense(g_two_b, back_down.T) * gelu_slope(pre_act)
    g_b_up = jnp.sum(g_pre, axis=0)
    g_pre_b = g_pre.astype(bf16)
    g_norm_one = g_resid_two + dense(g_pre_b, back_up.T)
    g_resid_one, g_gain_one, g_shift_one = norm_back(
        g_norm_one, normed_one, inv_one, back_gain_one.astype(f32)
    )
    g_one_b = g_resid_one.astype(bf16)
    g_b_out = jnp.sum(g_resid_one, axis=0)
    g_context = split_heads(dense(g_one_b, back_out.T).astype(bf16))
    probs_f = jnp.exp(masked_scores(q_heads, k_heads, segments, scale) - log_total)
    probs_b = probs_f.astype(bf16)
    g_probs = jnp.einsum("gqhe,gkhe->ghqk", g_context, v_heads, preferred_element_type=f32)
    delta = jnp.sum(probs_f * g_probs, axis=-1, keepdims=True)
    g_scores = (probs_f * (g_probs - delta) * scale).astype(bf16)
    g_queries = jnp.einsum(
        "ghqk,gkhe->gqhe", g_scores, k_heads, preferred_element_type=f32
    ).reshape(-1, width)
    g_keys = jnp.einsum("ghqk,gqhe->gkhe", g_scores, q_heads, preferred_element_type=f32).reshape(
        -1, width
    )
    g_values = jnp.einsum(
        "ghqk,gqhe->gkhe", probs_b, g_context, preferred_element_type=f32
    ).reshape(-1, width)
    g_b_query = jnp.sum(g_queries, axis=0)
    g_b_value = jnp.sum(g_values, axis=0)
    gq_b, gk_b, gv_b = (g_queries.astype(bf16), g_keys.astype(bf16), g_values.astype(bf16))
    grad_tokens = (
        g_resid_one
        + dense(gq_b, back_query.T)
        + dense(gk_b, back_key.T)
        + dense(gv_b, back_value.T)
    ).astype(bf16)
    columns = (
        lax.all_to_all(tokens, "shard", split_axis=1, concat_axis=0, tiled=True),
        lax.all_to_all(context, "shard", split_axis=1, concat_axis=0, tiled=True),
        lax.all_to_all(norm_one_b, "shard", split_axis=1, concat_axis=0, tiled=True),
        lax.all_to_all(act, "shard", split_axis=1, concat_axis=0, tiled=True),
    )
    gathered = (
        lax.all_gather(gq_b, "shard", axis=0, tiled=True),
        lax.all_gather(gk_b, "shard", axis=0, tiled=True),
        lax.all_gather(gv_b, "shard", axis=0, tiled=True),
        lax.all_gather(g_one_b, "shard", axis=0, tiled=True),
        lax.all_gather(g_pre_b, "shard", axis=0, tiled=True),
        lax.all_gather(g_two_b, "shard", axis=0, tiled=True),
    )
    vectors = (
        lax.psum_scatter(
            g_b_query.astype(jnp.bfloat16), "shard", scatter_dimension=0, tiled=True
        ).astype(jnp.float32),
        lax.psum_scatter(
            g_b_value.astype(jnp.bfloat16), "shard", scatter_dimension=0, tiled=True
        ).astype(jnp.float32),
        lax.psum_scatter(
            g_b_out.astype(jnp.bfloat16), "shard", scatter_dimension=0, tiled=True
        ).astype(jnp.float32),
        lax.psum_scatter(
            g_gain_one.astype(jnp.bfloat16), "shard", scatter_dimension=0, tiled=True
        ).astype(jnp.float32),
        lax.psum_scatter(
            g_shift_one.astype(jnp.bfloat16), "shard", scatter_dimension=0, tiled=True
        ).astype(jnp.float32),
        lax.psum_scatter(
            g_b_up.astype(jnp.bfloat16), "shard", scatter_dimension=0, tiled=True
        ).astype(jnp.float32),
        lax.psum_scatter(
            g_b_down.astype(jnp.bfloat16), "shard", scatter_dimension=0, tiled=True
        ).astype(jnp.float32),
        lax.psum_scatter(
            g_gain_two.astype(jnp.bfloat16), "shard", scatter_dimension=0, tiled=True
        ).astype(jnp.float32),
        lax.psum_scatter(
            g_shift_two.astype(jnp.bfloat16), "shard", scatter_dimension=0, tiled=True
        ).astype(jnp.float32),
    )
    own_query = dense(columns[0].T, gathered[0])
    own_key = dense(columns[0].T, gathered[1])
    own_value = dense(columns[0].T, gathered[2])
    own_out = dense(columns[1].T, gathered[3])
    own_up = dense(columns[2].T, gathered[4])
    own_down = dense(columns[3].T, gathered[5])
    summed = lax.psum(
        (
            own_query,
            own_key,
            own_value,
            own_out,
            vectors[0],
            vectors[1],
            vectors[2],
            vectors[3],
            vectors[4],
            own_up,
            vectors[5],
            own_down,
            vectors[6],
            vectors[7],
            vectors[8],
        ),
        "rep",
    )
    return (
        output,
        grad_tokens,
        summed[0],
        summed[1],
        summed[2],
        summed[3],
        summed[4],
        summed[5],
        summed[6],
        summed[7],
        summed[8],
        summed[9],
        summed[10],
        summed[11],
        summed[12],
        summed[13],
        summed[14],
    )


def solution(mesh):
    return jax.shard_map(
        body,
        mesh=mesh,
        in_specs=(
            P(("rep", "shard"), None),
            P(("rep", "shard"), None),
            P("shard", None),
            P("shard", None),
            P("shard", None),
            P("shard", None),
            P("shard"),
            P("shard"),
            P("shard"),
            P("shard"),
            P("shard"),
            P("shard", None),
            P("shard"),
            P("shard", None),
            P("shard"),
            P("shard"),
            P("shard"),
            P(("rep", "shard"), None),
        ),
        out_specs=(
            P(("rep", "shard"), None),
            P(("rep", "shard"), None),
            P("shard", None),
            P("shard", None),
            P("shard", None),
            P("shard", None),
            P("shard"),
            P("shard"),
            P("shard"),
            P("shard"),
            P("shard"),
            P("shard", None),
            P("shard"),
            P("shard", None),
            P("shard"),
            P("shard"),
            P("shard"),
        ),
        check_vma=False,
    )
```

profile of v0, /device:TPU:0, one launch (start us, length us, event | category | flops | bytes accessed | tf_op | source)
XLA Modules:
  0.0 633.8 jit_solution(14550670519471130721)
XLA Ops:
  12.1 6.3 %all-to-all-start = ((bf16[128,4,192]{0,2,1:T(8,128)(2,1)}), bf16[128,4,192]{0,2,1:T(8,128)(2,1)S(1)}, u32[]{:S(2)}, u32[]{:S(2)}) async-start(bf16[128,4,192]{0,2,1:T(8,128)(2,1)} %bitcast.19), calls=%async_computation | async-start | bytes 393216 | tf_op jit(solution)/shard_map/all_to_all | solution.py:186
  21.4 20.4 %all-reduce.20 = (bf16[768]{0:T(1024)(128)(2,1)S(1)}, bf16[768]{0:T(1024)(128)(2,1)S(1)}, bf16[768]{0:T(1024)(128)(2,1)S(1)}, bf16[768]{0:T(1024)(128)(2,1)S(1)}...) all-reduce(bf16[768]{0:T(1024)(128)(2,1)S(1)} %dynamic-update-slice, ...), channel_id=1, replica_groups=mesh['rep'=8,'shard'=4] {'shard'}, use_global_device_ids=true, to_apply=%add | all-reduce | flops 5376 | bytes 21504
  41.8 13.3 %all-gather = bf16[4,1,768]{2,1,0:T(2,128)(2,1)S(1)} all-gather(bf16[1,1,768]{2,1,0:T(2,128)(2,1)S(1)} %reshape.263), channel_id=1, replica_groups=mesh['rep'=8,'shard'=4] {'shard'}, dimensions={0}, use_global_device_ids=true | all-gather | bytes 7680 | tf_op jit(solution)/shard_map/all_gather | solution.py:84
  55.3 1.6 fusion.13
  57.0 19.7 %all-gather.13.cloned.1.call-done = bf16[768,768]{1,0:T(8,128)(2,1)} async-done(((bf16[192,768]{1,0:T(8,128)(2,1)}), bf16[768,768]{1,0:T(8,128)(2,1)}) %all-gather.13.cloned.1.call-update) | async-done | bytes 1179664 | tf_op jit(solution)/shard_map/all_gather | solution.py:75
  78.5 29.3 %all-gather.9.cloned.1.call-done = bf16[768,768]{1,0:T(8,128)(2,1)} async-done(((bf16[192,768]{1,0:T(8,128)(2,1)}), bf16[768,768]{1,0:T(8,128)(2,1)}) %all-gather.9.cloned.1.call-update) | async-done | bytes 1179664 | tf_op jit(solution)/shard_map/all_gather | solution.py:76
  107.9 1.6 fusion.12
  111.1 27.7 %all-gather.15.cloned.1.call-done = bf16[768,768]{1,0:T(8,128)(2,1)} async-done(((bf16[192,768]{1,0:T(8,128)(2,1)}), bf16[768,768]{1,0:T(8,128)(2,1)}) %all-gather.15.cloned.1.call-update) | async-done | bytes 1179664 | tf_op jit(solution)/shard_map/all_gather | solution.py:77
  138.8 1.8 fusion.60
  141.8 87.0 %all-gather.17.cloned.1.call-done = bf16[768,3072]{1,0:T(8,128)(2,1)} async-done(((bf16[192,3072]{1,0:T(8,128)(2,1)}), bf16[768,3072]{1,0:T(8,128)(2,1)}) %all-gather.17.cloned.1.call-update) | async-done | bytes 4718608 | tf_op jit(solution)/shard_map/all_gather | solution.py:83
  228.9 4.6 multiply_convert_fusion
  233.4 84.7 %all-gather.19.cloned.1.call-done = bf16[3072,768]{1,0:T(8,128)(2,1)} async-done(((bf16[768,768]{1,0:T(8,128)(2,1)}), bf16[3072,768]{1,0:T(8,128)(2,1)}) %all-gather.19.cloned.1.call-update) | async-done | bytes 4718608 | tf_op jit(solution)/shard_map/all_gather | solution.py:85
  318.1 3.4 fusion.61
  323.4 3.2 fusion.55
  326.6 5.0 multiply_reduce_fusion.1
  335.9 1.7 fusion.57
  338.4 34.3 %all_gather.79 = bf16[512,768]{0,1:T(8,128)(2,1)S(1)} all-gather(bf16[128,768]{0,1:T(8,128)(2,1)S(1)} %bitcast.132), channel_id=1, replica_groups=mesh['rep'=8,'shard'=4] {'shard'}, dimensions={0}, use_global_device_ids=true | all-gather | bytes 983040 | tf_op jit(solution)/shard_map/all_gather | solution.py:193
  372.7 10.4 %all-to-all-start.1 = ((bf16[128,4,192]{0,2,1:T(8,128)(2,1)}), bf16[128,4,192]{0,2,1:T(8,128)(2,1)}, u32[]{:S(2)}, u32[]{:S(2)}) async-start(bf16[128,4,192]{0,2,1:T(8,128)(2,1)} %bitcast.27), calls=%async_computation.1 | async-start | bytes 393216 | tf_op jit(solution)/shard_map/all_to_all | solution.py:187
  384.4 32.5 %all_gather.80 = bf16[512,768]{0,1:T(8,128)(2,1)S(1)} all-gather(bf16[128,768]{0,1:T(8,128)(2,1)S(1)} %bitcast.126), channel_id=1, replica_groups=mesh['rep'=8,'shard'=4] {'shard'}, dimensions={0}, use_global_device_ids=true | all-gather | bytes 983040 | tf_op jit(solution)/shard_map/all_gather | solution.py:194
  416.9 17.8 %all_gather.78 = bf16[512,768]{0,1:T(8,128)(2,1)S(1)} all-gather(bf16[128,768]{0,1:T(8,128)(2,1)} %bitcast.134), channel_id=1, replica_groups=mesh['rep'=8,'shard'=4] {'shard'}, dimensions={0}, use_global_device_ids=true | all-gather | bytes 983040 | tf_op jit(solution)/shard_map/all_gather | solution.py:192
  434.7 3.5 all-to-all-start.3
  440.6 30.5 %all_gather.81 = bf16[512,768]{1,0:T(8,128)(2,1)S(1)} all-gather(bf16[128,768]{1,0:T(8,128)(2,1)S(1)} %copy-done.8), channel_id=1, replica_groups=mesh['rep'=8,'shard'=4] {'shard'}, dimensions={0}, use_global_device_ids=true | all-gather | bytes 983040 | tf_op jit(solution)/shard_map/all_gather | solution.py:195
  471.1 2.1 fusion.37
  473.2 17.2 %all_gather.83 = bf16[512,768]{1,0:T(8,128)(2,1)S(1)} all-gather(bf16[128,768]{1,0:T(8,128)(2,1)S(1)} %copy-done.19), channel_id=1, replica_groups=mesh['rep'=8,'shard'=4] {'shard'}, dimensions={0}, use_global_device_ids=true | all-gather | bytes 983040 | tf_op jit(solution)/shard_map/all_gather | solution.py:197
  490.4 5.3 all-to-all-start.2
  495.8 2.2 fusion.65
  498.0 4.0 all-to-all-done.2
  502.0 4.1 fusion.34
  512.3 18.8 %all-reduce.19 = (bf16[768]{0:T(1024)(128)(2,1)}, bf16[768]{0:T(1024)(128)(2,1)}, bf16[768]{0:T(1024)(128)(2,1)}, bf16[768]{0:T(1024)(128)(2,1)}, bf16[768]{0:T(...) all-reduce(bf16[768]{0:T(1024)(128)(2,1)} %dynamic-update-slice.7, ...), channel_id=1, replica_groups=mesh['rep'=8,'shard'=4] {'shard'}, use_global_device_ids=true, to_apply=%add.7 | all-reduce | flops 9984 | bytes 39936
  543.1 23.2 %all-reduce.17 = (f32[192]{0:T(256)}, f32[192]{0:T(256)}, f32[192]{0:T(256)}, f32[192]{0:T(256)}, f32[192]{0:T(256)}, /*index=5*/f32[768]{0:T(1024)}, f32[192]{0:T(256)}, f32[192]{0:T(256)}, f32[192]{0:T(256)}) all-reduce(f32[192]{0:T(256)} %dynamic-slice_convert_fusion.8, ...), channel_id=1, replica_groups=mesh['rep'=8,'shard'=4] {'rep'}, use_global_device_ids=true, to_apply=%region_17.18 | all-reduce | flops 2304 | bytes 18432 | tf_op jit(solution)/shard_map/psum | solution.py:234
  571.9 46.6 %all-reduce.23.cloned.1.call-done = (f32[192,768]{1,0:T(8,128)}, f32[192,768]{1,0:T(8,128)}, f32[192,768]{1,0:T(8,128)}, f32[192,768]{1,0:T(8,128)}, f32[192,3072]{1,0:T(8,128)}, /*index=5*/f32[768,768]{1,0:T(8,128)}) async-done(((f32[192,768]{1,0:T(8,128)}, f32[192,768]{1,0:T(8,128)}, f32[192,768]{1,0:T(8,128)}, f32[192,768]{1,0:T(8,128)}, f32[192,3072]{1,0:T(8,128)}, /*index=5*/f32[768,768]{1,0:T(8,128)}), ...) | async-done | bytes 7077904 | tf_op jit(solution)/shard_map/psum | solution.py:234
  618.5 2.0 copy.120
  (187 shorter events, 51.1 us)
Async XLA Ops:
  7.2 48.1 %all-gather.11.cloned.1.call-start = ((), (), s32[]{:S(2)}) async-start(), calls=%async_computation.5 | async-start | bytes 1474560 | tf_op jit(solution)/shard_map/all_gather | solution.py:74
  7.9 68.8 %all-gather.13.cloned.1.call-start = ((), (), s32[]{:S(2)}) async-start(), calls=%async_computation.6 | async-start | bytes 1474560 | tf_op jit(solution)/shard_map/all_gather | solution.py:75
  8.7 99.2 %all-gather.9.cloned.1.call-start = ((), (), s32[]{:S(2)}) async-start(), calls=%async_computation.4 | async-start | bytes 1474560 | tf_op jit(solution)/shard_map/all_gather | solution.py:76
  9.4 129.4 %all-gather.15.cloned.1.call-start = ((), (), s32[]{:S(2)}) async-start(), calls=%async_computation.7 | async-start | bytes 1474560 | tf_op jit(solution)/shard_map/all_gather | solution.py:77
  10.0 8.4 %copy-start.30 = (u32[32]{0:T(128)S(1)}, u32[32]{0:T(128)}, u32[]{:S(2)}) copy-start(u32[32]{0:T(128)} %constant.35) | copy-start | bytes 388
  10.0 9.7 %copy-start.32 = (bf16[192]{0:T(256)(128)(2,1)S(1)}, bf16[192]{0:T(256)(128)(2,1)}, u32[]{:S(2)}) copy-start(bf16[192]{0:T(256)(128)(2,1)} %param.25) | copy-start | bytes 1156
  10.0 9.9 %copy-start.33 = (bf16[192]{0:T(256)(128)(2,1)S(1)}, bf16[192]{0:T(256)(128)(2,1)}, u32[]{:S(2)}) copy-start(bf16[192]{0:T(256)(128)(2,1)} %param.24) | copy-start | bytes 1156
  10.0 10.2 %copy-start.34 = (bf16[192]{0:T(256)(128)(2,1)S(1)}, bf16[192]{0:T(256)(128)(2,1)}, u32[]{:S(2)}) copy-start(bf16[192]{0:T(256)(128)(2,1)} %param.26) | copy-start | bytes 1156
  10.0 10.4 %copy-start.35 = (bf16[192]{0:T(256)(128)(2,1)S(1)}, bf16[192]{0:T(256)(128)(2,1)}, u32[]{:S(2)}) copy-start(bf16[192]{0:T(256)(128)(2,1)} %param.27) | copy-start | bytes 1156
  10.1 10.6 %copy-start.36 = (bf16[192]{0:T(256)(128)(2,1)S(1)}, bf16[192]{0:T(256)(128)(2,1)}, u32[]{:S(2)}) copy-start(bf16[192]{0:T(256)(128)(2,1)} %param.28) | copy-start | bytes 1156
  10.1 10.8 %copy-start.37 = (bf16[192]{0:T(256)(128)(2,1)S(1)}, bf16[192]{0:T(256)(128)(2,1)}, u32[]{:S(2)}) copy-start(bf16[192]{0:T(256)(128)(2,1)} %param.32) | copy-start | bytes 1156
  10.1 11.1 %copy-start.38 = (bf16[192]{0:T(256)(128)(2,1)S(1)}, bf16[192]{0:T(256)(128)(2,1)}, u32[]{:S(2)}) copy-start(bf16[192]{0:T(256)(128)(2,1)} %param.33) | copy-start | bytes 1156
  10.1 31.7 %copy-start.31 = (bf16[768]{0:T(1024)(128)(2,1)S(1)}, bf16[768]{0:T(1024)(128)(2,1)}, u32[]{:S(2)}) copy-start(bf16[768]{0:T(1024)(128)(2,1)} %param.30) | copy-start | bytes 4612
  10.1 45.0 %copy-start.29 = (s32[1,128]{1,0:T(1,128)S(1)}, s32[1,128]{1,0:T(1,128)}, u32[]{:S(2)}) copy-start(s32[1,128]{1,0:T(1,128)} %param.19) | copy-start | bytes 1540
  10.1 218.8 %all-gather.17.cloned.1.call-start = ((), (), s32[]{:S(2)}) async-start(), calls=%async_computation.8 | async-start | bytes 5898240 | tf_op jit(solution)/shard_map/all_gather | solution.py:83
  10.7 307.4 %all-gather.19.cloned.1.call-start = ((), (), s32[]{:S(2)}) async-start(), calls=%async_computation.9 | async-start | bytes 5898240 | tf_op jit(solution)/shard_map/all_gather | solution.py:85
  12.1 360.6 %all-to-all-start = ((bf16[128,4,192]{0,2,1:T(8,128)(2,1)}), bf16[128,4,192]{0,2,1:T(8,128)(2,1)S(1)}, u32[]{:S(2)}, u32[]{:S(2)}) async-start(bf16[128,4,192]{0,2,1:T(8,128)(2,1)} %bitcast.19), calls=%async_computation | async-start | bytes 393216 | tf_op jit(solution)/shard_map/all_to_all | solution.py:186
  18.4 483.6 %all-gather.21.cloned.1.call-start = ((), (), s32[]{:S(2)}) async-start(), calls=%async_computation.10 | async-start | bytes 3932160 | tf_op jit(solution)/shard_map/all_gather | solution.py:196
  57.0 52.6 %copy-start.12 = (bf16[128,768]{0,1:T(8,128)(2,1)}, bf16[128,768]{0,1:T(8,128)(2,1)S(1)}, u32[]{:S(2)}) copy-start(bf16[128,768]{0,1:T(8,128)(2,1)S(1)} %copy.62) | copy-start | bytes 589828
  78.5 31.5 %copy-start.14 = (bf16[128,768]{0,1:T(8,128)(2,1)}, bf16[128,768]{0,1:T(8,128)(2,1)S(1)}, u32[]{:S(2)}) copy-start(bf16[128,768]{0,1:T(8,128)(2,1)S(1)} %copy.63) | copy-start | bytes 589828
  140.7 185.9 %copy-start.23 = (f32[128]{0:T(128)}, f32[128]{0:T(128)S(1)}, u32[]{:S(2)}) copy-start(f32[128]{0:T(128)S(1)} %broadcast_multiply_fusion.5) | copy-start | bytes 1540
  140.9 185.7 %copy-start.26 = (f32[128]{0:T(128)}, f32[128]{0:T(128)S(1)}, u32[]{:S(2)}) copy-start(f32[128]{0:T(128)S(1)} %add_rsqrt_fusion.1) | copy-start | bytes 1540
  337.9 46.4 %copy-start.16 = (bf16[12,64,128]{2,1,0:T(8,128)(2,1)}, bf16[12,64,128]{2,1,0:T(8,128)(2,1)S(1)}, u32[]{:S(2)}) copy-start(bf16[12,64,128]{2,1,0:T(8,128)(2,1)S(1)} %convolution_convert_fusion) | copy-start | bytes 589828
  372.7 62.0 %all-to-all-start.1 = ((bf16[128,4,192]{0,2,1:T(8,128)(2,1)}), bf16[128,4,192]{0,2,1:T(8,128)(2,1)}, u32[]{:S(2)}, u32[]{:S(2)}) async-start(bf16[128,4,192]{0,2,1:T(8,128)(2,1)} %bitcast.27), calls=%async_computation.1 | async-start | bytes 393216 | tf_op jit(solution)/shard_map/all_to_all | solution.py:187
  434.7 55.8 %all-to-all-start.3 = ((bf16[128,4,768]{2,0,1:T(8,128)(2,1)}), bf16[128,4,768]{2,0,1:T(8,128)(2,1)S(1)}, u32[]{:S(2)}, u32[]{:S(2)}) async-start(bf16[128,4,768]{2,0,1:T(8,128)(2,1)} %bitcast.117), calls=%async_computation.3 | async-start | bytes 1572864 | tf_op jit(solution)/shard_map/all_to_all | solution.py:189
  440.6 32.5 %copy-start.19 = (bf16[128,768]{1,0:T(8,128)(2,1)S(1)}, bf16[128,768]{1,0:T(8,128)(2,1)}, u32[]{:S(2)}) copy-start(bf16[128,768]{1,0:T(8,128)(2,1)} %copy-done.18) | copy-start | bytes 589828
  490.4 11.6 %all-to-all-start.2 = ((bf16[128,4,192]{0,2,1:T(8,128)(2,1)}), bf16[128,4,192]{0,2,1:T(8,128)(2,1)S(1)}, u32[]{:S(2)}, u32[]{:S(2)}) async-start(bf16[128,4,192]{0,2,1:T(8,128)(2,1)} %bitcast.31), calls=%async_computation.2 | async-start | bytes 393216 | tf_op jit(solution)/shard_map/all_to_all | solution.py:188
  495.8 122.7 %all-reduce.23.cloned.1.call-start = ((), (), s32[]{:S(2)}) async-start(), calls=%async_computation.11 | async-start | bytes 14155776 | tf_op jit(solution)/shard_map/psum | solution.py:234
  506.1 60.2 %copy-start.25 = (f32[128]{0:T(128)S(1)}, f32[128]{0:T(128)}, u32[]{:S(2)}) copy-start(f32[128]{0:T(128)} %copy-done.24) | copy-start | bytes 1540
  506.1 61.7 %copy-start.1 = (bf16[768,768]{1,0:T(8,128)(2,1)S(1)}, bf16[768,768]{1,0:T(8,128)(2,1)}, u32[]{:S(2)}) copy-start(bf16[768,768]{1,0:T(8,128)(2,1)} %all-gather.11.cloned.1.call-done) | copy-start | bytes 3538948
  507.0 62.3 %copy-start.2 = (bf16[768,768]{1,0:T(8,128)(2,1)S(1)}, bf16[768,768]{1,0:T(8,128)(2,1)}, u32[]{:S(2)}) copy-start(bf16[768,768]{1,0:T(8,128)(2,1)} %all-gather.13.cloned.1.call-done) | copy-start | bytes 3538948
  507.6 61.7 %copy-start.17 = (bf16[12,64,128]{2,1,0:T(8,128)(2,1)S(1)}, bf16[12,64,128]{2,1,0:T(8,128)(2,1)}, u32[]{:S(2)}) copy-start(bf16[12,64,128]{2,1,0:T(8,128)(2,1)} %copy-done.16) | copy-start | bytes 589828
  (21 other events, 63.3 us)
Sparse Core Ops, SparseCore 0:
  9.6 36.2 all-gather.10
  47.4 29.3 all-gather.12
  78.3 29.4 all-gather.8
  109.3 29.4 all-gather.14
  140.2 88.6 all-gather.16
  230.3 87.7 all-gather.18
  326.7 91.0 all-gather.20
  506.2 112.1 all-reduce.22
where the time goes:
time: 635 us; the launch traced here: 634 us
  waiting for transfers between devices  303 us (48%)
  blocking collectives  208 us (33%)
  matrix products  42.7 us (7%)
  starting transfers between devices  25.8 us (4%)
  local copies, waits for them, and re-layouts  19.8 us (3%)
  other arithmetic  17.9 us (3%)
  between operations  16.7 us (3%)
    all_gather x1, waiting for transfers between devices, body(): lax.all_gather(w_up, 'shard', axis=0, tiled=True)  87 us
    all_gather x1, waiting for transfers between devices, body(): lax.all_gather(w_down, 'shard', axis=0, tiled=True)  84.7 us
    psum x1, waiting for transfers between devices, body(): lax.psum((own_query, own_key, own_value, own_out, vectors[0], vectors[1],...  46.6 us
    unnamed x2, blocking collectives  39.2 us
    dot_general x18, matrix products, dense(): return jnp.dot(left, right, preferred_element_type=jnp.float32)  38.6 us
    all_gather x1, blocking collectives, body(): lax.all_gather(gk_b, 'shard', axis=0, tiled=True)  34.3 us
    all_gather x1, blocking collectives, body(): lax.all_gather(gv_b, 'shard', axis=0, tiled=True)  32.5 us
    all_gather x1, blocking collectives, body(): lax.all_gather(g_one_b, 'shard', axis=0, tiled=True)  30.5 us
  transfers between devices with their start and end apart: 12, of which 7 were waited for; matrix products, arithmetic and copies ran while one was open for 10% of the time, Pallas kernels for 0%

commit v1 on v0

--- a/solution.py
+++ b/solution.py
@@ -9,6 +9,19 @@
 masked_value = -1e30
 root_half = 0.7071067811865476
 inv_root_tau = 0.3989422804014327
+
+
+def collect(value, axis, dim):
+    ways = lax.axis_size(axis)
+    up = [(d, (d + 1) % ways) for d in range(ways)]
+    down = [(d, (d - 1) % ways) for d in range(ways)]
+    earlier, later = ([value], [value])
+    for _ in range(ways // 2):
+        earlier.append(lax.ppermute(earlier[-1], axis, up))
+    for _ in range((ways - 1) // 2):
+        later.append(lax.ppermute(later[-1], axis, down))
+    line = jnp.concatenate([*earlier[::-1], *later[1:]], axis=dim)
+    return jnp.roll(line, (lax.axis_index(axis) - ways // 2) * value.shape[dim], axis=dim)
 
 
 def layer_norm(hidden, gain, shift):
@@ -82,7 +95,7 @@
         lax.all_gather(shift_one, "shard", axis=0, tiled=True),
         lax.all_gather(w_up, "shard", axis=0, tiled=True),
         lax.all_gather(b_up, "shard", axis=0, tiled=True),
-        lax.all_gather(w_down, "shard", axis=0, tiled=True),
+        collect(w_down, "shard", 0),
         lax.all_gather(b_down, "shard", axis=0, tiled=True),
         lax.all_gather(gain_two, "shard", axis=0, tiled=True),
         lax.all_gather(shift_two, "shard", axis=0, tiled=True),

time: 635 us -> 601 us (0.946)
  waiting for transfers between devices: 303 us -> 177 us
  blocking collectives: 208 us -> 277 us
  local copies, waits for them, and re-layouts: 19.8 us -> 36.5 us
    all_gather x1 -> x0, waiting for transfers between devices: 84.7 us -> none  [body(): lax.all_gather(w_down, 'shard', axis=0, tiled=True)]
    unnamed x2, blocking collectives: 39.2 us -> 109 us
    all_gather x1, waiting for transfers between devices: 19.7 us -> 0.02 us  [body(): lax.all_gather(w_key, 'shard', axis=0, tiled=True)]
    all_gather x1, waiting for transfers between devices: 87 us -> 70.3 us  [body(): lax.all_gather(w_up, 'shard', axis=0, tiled=True)]
    unnamed x107 -> x110, local copies, waits for them, and re-layouts: 15.9 us -> 30.2 us
  transfers between devices with their start and end apart: 12 -> 14, of which waited for: 7 -> 5; matrix products, arithmetic and copies ran while one was open for 10% -> 14% of each run, Pallas kernels for 0% -> 0%
where the time goes in v1:
time: 601 us; the launch traced here: 600 us
  blocking collectives  277 us (46%)
  waiting for transfers between devices  177 us (29%)
  matrix products  45.1 us (8%)
  local copies, waits for them, and re-layouts  36.5 us (6%)
  starting transfers between devices  28.5 us (5%)
  other arithmetic  17.9 us (3%)
  between operations  16.8 us (3%)
    unnamed x2, blocking collectives  109 us
    all_gather x1, waiting for transfers between devices, body(): lax.all_gather(w_up, 'shard', axis=0, tiled=True)  70.3 us
    psum x1, waiting for transfers between devices, body(): lax.psum((own_query, own_key, own_value, own_out, vectors[0], vectors[1],...  46.7 us
    dot_general x18, matrix products, dense(): return jnp.dot(left, right, preferred_element_type=jnp.float32)  41 us
    all_gather x1, blocking collectives, body(): lax.all_gather(gk_b, 'shard', axis=0, tiled=True)  34.2 us
    all_gather x1, blocking collectives, body(): lax.all_gather(gv_b, 'shard', axis=0, tiled=True)  32.6 us
    all_gather x1, blocking collectives, body(): lax.all_gather(g_one_b, 'shard', axis=0, tiled=True)  30.5 us
    unnamed x110, local copies, waits for them, and re-layouts  30.2 us
  transfers between devices with their start and end apart: 14, of which 5 were waited for; matrix products, arithmetic and copies ran while one was open for 14% of the time, Pallas kernels for 0%

profile of v1, /device:TPU:0, one launch (start us, length us, event | category | flops | bytes accessed | tf_op | source)
XLA Modules:
  0.0 599.6 jit_solution(17770590414227226327)
XLA Ops:
  10.7 3.1 collective-permute-start
  13.8 2.1 collective-permute-start.2
  16.7 3.4 all-to-all-start
  23.1 89.8 %all-reduce.20 = (bf16[768]{0:T(1024)(128)(2,1)S(1)}, bf16[768]{0:T(1024)(128)(2,1)S(1)}, bf16[768]{0:T(1024)(128)(2,1)S(1)}, bf16[768]{0:T(1024)(128)(2,1)S(1)}...) all-reduce(bf16[768]{0:T(1024)(128)(2,1)S(1)} %dynamic-update-slice, ...), channel_id=1, replica_groups=mesh['rep'=8,'shard'=4] {'shard'}, use_global_device_ids=true, to_apply=%add | all-reduce | flops 5376 | bytes 21504
  112.9 13.3 %all-gather = bf16[4,1,768]{2,1,0:T(2,128)(2,1)S(1)} all-gather(bf16[1,1,768]{2,1,0:T(2,128)(2,1)S(1)} %reshape.263), channel_id=1, replica_groups=mesh['rep'=8,'shard'=4] {'shard'}, dimensions={0}, use_global_device_ids=true | all-gather | bytes 7680 | tf_op jit(solution)/shard_map/all_gather | solution.py:97
  130.3 24.4 %all-gather.8.cloned.1.call-done = bf16[768,768]{1,0:T(8,128)(2,1)} async-done(((bf16[192,768]{1,0:T(8,128)(2,1)}), bf16[768,768]{1,0:T(8,128)(2,1)}) %all-gather.8.cloned.1.call-update) | async-done | bytes 1179664 | tf_op jit(solution)/shard_map/all_gather | solution.py:89
  157.9 28.9 %all-gather.14.cloned.1.call-done = bf16[768,768]{1,0:T(8,128)(2,1)} async-done(((bf16[192,768]{1,0:T(8,128)(2,1)}), bf16[768,768]{1,0:T(8,128)(2,1)}) %all-gather.14.cloned.1.call-update) | async-done | bytes 1179664 | tf_op jit(solution)/shard_map/all_gather | solution.py:90
  189.8 2.4 constant_dynamic-update-slice_fusion.7
  192.2 2.4 constant_dynamic-update-slice_fusion.6
  195.7 2.5 constant_dynamic-update-slice_fusion.4
  198.2 2.4 constant_dynamic-update-slice_fusion.3
  200.6 2.4 constant_dynamic-update-slice_fusion.2
  204.1 2.5 constant_dynamic-update-slice_fusion
  206.6 70.3 %all-gather.16.cloned.1.call-done = bf16[768,3072]{1,0:T(8,128)(2,1)} async-done(((bf16[192,3072]{1,0:T(8,128)(2,1)}), bf16[768,3072]{1,0:T(8,128)(2,1)}) %all-gather.16.cloned.1.call-update) | async-done | bytes 4718608 | tf_op jit(solution)/shard_map/all_gather | solution.py:96
  276.8 3.5 multiply_convert_fusion
  280.3 4.0 fusion.75
  286.1 6.0 %fusion.69 = (bf16[3072]{0:T(1024)(128)(2,1)}, bf16[128,3072]{1,0:T(8,128)(2,1)}) fusion(f32[128,3072]{1,0:T(8,128)S(1)} %get-tuple-element.73, bf16[128,768]{1,0:T(8,128)(2,1)S(1)} %convert_element_type.189, bf16[6144,768]{1,0:T(8,128)(2,1)} %constant_dynamic-update-slice_fusion, s32[]{:T(128)S(6)} %select_n.21), kind=kOutput, calls=%fused_computation.120 | convolution fusion | flops 608302080 | bytes 7280644 | tf_op jit(solution)/shard_map/dot_general | solution.py:61
  292.2 5.0 multiply_reduce_fusion.1
  304.0 34.2 %all_gather.75 = bf16[512,768]{0,1:T(8,128)(2,1)S(1)} all-gather(bf16[128,768]{0,1:T(8,128)(2,1)S(1)} %bitcast.128), channel_id=1, replica_groups=mesh['rep'=8,'shard'=4] {'shard'}, dimensions={0}, use_global_device_ids=true | all-gather | bytes 983040 | tf_op jit(solution)/shard_map/all_gather | solution.py:206
  338.2 10.5 %all-to-all-start.1 = ((bf16[128,4,192]{0,2,1:T(8,128)(2,1)}), bf16[128,4,192]{0,2,1:T(8,128)(2,1)}, u32[]{:S(2)}, u32[]{:S(2)}) async-start(bf16[128,4,192]{0,2,1:T(8,128)(2,1)} %bitcast.27), calls=%async_computation.1 | async-start | bytes 393216 | tf_op jit(solution)/shard_map/all_to_all | solution.py:200
  349.9 32.6 %all_gather.76 = bf16[512,768]{0,1:T(8,128)(2,1)S(1)} all-gather(bf16[128,768]{0,1:T(8,128)(2,1)S(1)} %bitcast.122), channel_id=1, replica_groups=mesh['rep'=8,'shard'=4] {'shard'}, dimensions={0}, use_global_device_ids=true | all-gather | bytes 983040 | tf_op jit(solution)/shard_map/all_gather | solution.py:207
  382.5 17.8 %all_gather.74 = bf16[512,768]{0,1:T(8,128)(2,1)S(1)} all-gather(bf16[128,768]{0,1:T(8,128)(2,1)} %bitcast.130), channel_id=1, replica_groups=mesh['rep'=8,'shard'=4] {'shard'}, dimensions={0}, use_global_device_ids=true | all-gather | bytes 983040 | tf_op jit(solution)/shard_map/all_gather | solution.py:205
  400.2 3.7 all-to-all-start.3
  406.4 30.5 %all_gather.77 = bf16[512,768]{1,0:T(8,128)(2,1)S(1)} all-gather(bf16[128,768]{1,0:T(8,128)(2,1)S(1)} %copy-done.9), channel_id=1, replica_groups=mesh['rep'=8,'shard'=4] {'shard'}, dimensions={0}, use_global_device_ids=true | all-gather | bytes 983040 | tf_op jit(solution)/shard_map/all_gather | solution.py:208
  439.0 17.2 %all_gather.79 = bf16[512,768]{1,0:T(8,128)(2,1)S(1)} all-gather(bf16[128,768]{1,0:T(8,128)(2,1)S(1)} %copy-done.19), channel_id=1, replica_groups=mesh['rep'=8,'shard'=4] {'shard'}, dimensions={0}, use_global_device_ids=true | all-gather | bytes 983040 | tf_op jit(solution)/shard_map/all_gather | solution.py:210
  456.2 5.3 all-to-all-start.2
  461.6 2.2 fusion.79
  463.8 4.0 all-to-all-done.2
  467.8 4.1 fusion.46
  478.2 18.8 %all-reduce.19 = (bf16[768]{0:T(1024)(128)(2,1)}, bf16[768]{0:T(1024)(128)(2,1)}, bf16[768]{0:T(1024)(128)(2,1)}, bf16[768]{0:T(1024)(128)(2,1)}, bf16[768]{0:T(...) all-reduce(bf16[768]{0:T(1024)(128)(2,1)} %dynamic-update-slice.7, ...), channel_id=1, replica_groups=mesh['rep'=8,'shard'=4] {'shard'}, use_global_device_ids=true, to_apply=%add.7 | all-reduce | flops 9984 | bytes 39936
  508.9 23.2 %all-reduce.17 = (f32[192]{0:T(256)}, f32[192]{0:T(256)}, f32[192]{0:T(256)}, f32[192]{0:T(256)}, f32[192]{0:T(256)}, /*index=5*/f32[768]{0:T(1024)}, f32[192]{0:T(256)}, f32[192]{0:T(256)}, f32[192]{0:T(256)}) all-reduce(f32[192]{0:T(256)} %dynamic-slice_convert_fusion.8, ...), channel_id=1, replica_groups=mesh['rep'=8,'shard'=4] {'rep'}, use_global_device_ids=true, to_apply=%region_17.18 | all-reduce | flops 2304 | bytes 18432 | tf_op jit(solution)/shard_map/psum | solution.py:247
  537.6 46.7 %all-reduce.23.cloned.1.call-done = (f32[192,768]{1,0:T(8,128)}, f32[192,768]{1,0:T(8,128)}, f32[192,768]{1,0:T(8,128)}, f32[192,768]{1,0:T(8,128)}, f32[192,3072]{1,0:T(8,128)}, /*index=5*/f32[768,768]{1,0:T(8,128)}) async-done(((f32[192,768]{1,0:T(8,128)}, f32[192,768]{1,0:T(8,128)}, f32[192,768]{1,0:T(8,128)}, f32[192,768]{1,0:T(8,128)}, f32[192,3072]{1,0:T(8,128)}, /*index=5*/f32[768,768]{1,0:T(8,128)}), ...) | async-done | bytes 7077904 | tf_op jit(solution)/shard_map/psum | solution.py:247
  (193 shorter events, 63.9 us)
Async XLA Ops:
  7.2 14.4 %copy-start.33 = (bf16[192]{0:T(256)(128)(2,1)S(1)}, bf16[192]{0:T(256)(128)(2,1)}, u32[]{:S(2)}) copy-start(bf16[192]{0:T(256)(128)(2,1)} %param.24) | copy-start | bytes 1156
  7.2 14.7 %copy-start.34 = (bf16[192]{0:T(256)(128)(2,1)S(1)}, bf16[192]{0:T(256)(128)(2,1)}, u32[]{:S(2)}) copy-start(bf16[192]{0:T(256)(128)(2,1)} %param.26) | copy-start | bytes 1156
  7.3 14.9 %copy-start.35 = (bf16[192]{0:T(256)(128)(2,1)S(1)}, bf16[192]{0:T(256)(128)(2,1)}, u32[]{:S(2)}) copy-start(bf16[192]{0:T(256)(128)(2,1)} %param.27) | copy-start | bytes 1156
  7.3 15.1 %copy-start.36 = (bf16[192]{0:T(256)(128)(2,1)S(1)}, bf16[192]{0:T(256)(128)(2,1)}, u32[]{:S(2)}) copy-start(bf16[192]{0:T(256)(128)(2,1)} %param.28) | copy-start | bytes 1156
  7.3 15.3 %copy-start.37 = (bf16[192]{0:T(256)(128)(2,1)S(1)}, bf16[192]{0:T(256)(128)(2,1)}, u32[]{:S(2)}) copy-start(bf16[192]{0:T(256)(128)(2,1)} %param.32) | copy-start | bytes 1156
  7.3 15.6 %copy-start.38 = (bf16[192]{0:T(256)(128)(2,1)S(1)}, bf16[192]{0:T(256)(128)(2,1)}, u32[]{:S(2)}) copy-start(bf16[192]{0:T(256)(128)(2,1)} %param.33) | copy-start | bytes 1156
  7.3 105.6 %copy-start.31 = (bf16[768]{0:T(1024)(128)(2,1)S(1)}, bf16[768]{0:T(1024)(128)(2,1)}, u32[]{:S(2)}) copy-start(bf16[768]{0:T(1024)(128)(2,1)} %param.30) | copy-start | bytes 4612
  7.3 119.4 %all-gather.10.cloned.1.call-start = ((), (), s32[]{:S(2)}) async-start(), calls=%async_computation.5 | async-start | bytes 1474560 | tf_op jit(solution)/shard_map/all_gather | solution.py:87
  8.0 118.3 %copy-start.29 = (s32[1,128]{1,0:T(1,128)S(1)}, s32[1,128]{1,0:T(1,128)}, u32[]{:S(2)}) copy-start(s32[1,128]{1,0:T(1,128)} %param.19) | copy-start | bytes 1540
  8.1 120.4 %all-gather.12.cloned.1.call-start = ((), (), s32[]{:S(2)}) async-start(), calls=%async_computation.6 | async-start | bytes 1474560 | tf_op jit(solution)/shard_map/all_gather | solution.py:88
  8.8 145.9 %all-gather.8.cloned.1.call-start = ((), (), s32[]{:S(2)}) async-start(), calls=%async_computation.4 | async-start | bytes 1474560 | tf_op jit(solution)/shard_map/all_gather | solution.py:89
  9.5 177.2 %all-gather.14.cloned.1.call-start = ((), (), s32[]{:S(2)}) async-start(), calls=%async_computation.7 | async-start | bytes 1474560 | tf_op jit(solution)/shard_map/all_gather | solution.py:90
  10.1 266.7 %all-gather.16.cloned.1.call-start = ((), (), s32[]{:S(2)}) async-start(), calls=%async_computation.8 | async-start | bytes 5898240 | tf_op jit(solution)/shard_map/all_gather | solution.py:96
  10.7 115.7 %collective-permute-start = (bf16[768,768]{1,0:T(8,128)(2,1)S(1)}, bf16[768,768]{1,0:T(8,128)(2,1)}, u32[]{:S(2)}, u32[]{:S(2)}) collective-permute-start(bf16[768,768]{1,0:T(8,128)(2,1)S(1)} %copy-done.1), channel_id=1, source_target_pairs={{0,1},{1,2},{2,3},{3,0},{4,5},{5,6},{6,7},{7,4},{8,9},{9,10},{10,1... | collective-permute-start | bytes 3538952 | tf_op jit(solution)/shard_map/ppermute | solution.py:20
  13.8 181.9 %collective-permute-start.2 = (bf16[768,768]{1,0:T(8,128)(2,1)S(1)}, bf16[768,768]{1,0:T(8,128)(2,1)}, u32[]{:S(2)}, u32[]{:S(2)}) collective-permute-start(bf16[768,768]{1,0:T(8,128)(2,1)S(1)} %copy-done.1), channel_id=1, source_target_pairs={{0,3},{1,0},{2,1},{3,2},{4,7},{5,4},{6,5},{7,6},{8,11},{9,8},{10,9... | collective-permute-start | bytes 3538952 | tf_op jit(solution)/shard_map/ppermute | solution.py:22
  16.7 321.5 %all-to-all-start = ((bf16[128,4,192]{0,2,1:T(8,128)(2,1)}), bf16[128,4,192]{0,2,1:T(8,128)(2,1)S(1)}, u32[]{:S(2)}, u32[]{:S(2)}) async-start(bf16[128,4,192]{0,2,1:T(8,128)(2,1)} %bitcast.19), calls=%async_computation | async-start | bytes 393216 | tf_op jit(solution)/shard_map/all_to_all | solution.py:199
  20.1 447.7 %all-gather.18.cloned.1.call-start = ((), (), s32[]{:S(2)}) async-start(), calls=%async_computation.9 | async-start | bytes 3932160 | tf_op jit(solution)/shard_map/all_gather | solution.py:209
  126.4 63.4 %collective-permute-start.1 = (bf16[768,768]{1,0:T(8,128)(2,1)}, bf16[768,768]{1,0:T(8,128)(2,1)}, u32[]{:S(2)}, u32[]{:S(2)}) collective-permute-start(bf16[768,768]{1,0:T(8,128)(2,1)} %collective-permute-done), channel_id=1, source_target_pairs={{0,1},{1,2},{2,3},{3,0},{4,5},{5,6},{6,7},{7,4},{8,9},{9,10},{10,1... | collective-permute-start | bytes 3538952 | tf_op jit(solution)/shard_map/ppermute | solution.py:20
  128.5 28.0 %copy-start.12 = (bf16[128,768]{0,1:T(8,128)(2,1)}, bf16[128,768]{0,1:T(8,128)(2,1)S(1)}, u32[]{:S(2)}) copy-start(bf16[128,768]{0,1:T(8,128)(2,1)S(1)} %copy.62) | copy-start | bytes 589828
  130.3 26.5 %copy-start.14 = (bf16[128,768]{0,1:T(8,128)(2,1)}, bf16[128,768]{0,1:T(8,128)(2,1)S(1)}, u32[]{:S(2)}) copy-start(bf16[128,768]{0,1:T(8,128)(2,1)S(1)} %copy.63) | copy-start | bytes 589828
  188.6 103.6 %copy-start.23 = (f32[128]{0:T(128)}, f32[128]{0:T(128)S(1)}, u32[]{:S(2)}) copy-start(f32[128]{0:T(128)S(1)} %broadcast_multiply_fusion.5) | copy-start | bytes 1540
  188.8 103.4 %copy-start.26 = (f32[128]{0:T(128)}, f32[128]{0:T(128)S(1)}, u32[]{:S(2)}) copy-start(f32[128]{0:T(128)S(1)} %add_rsqrt_fusion.1) | copy-start | bytes 1540
  303.5 46.4 %copy-start.16 = (bf16[12,64,128]{2,1,0:T(8,128)(2,1)}, bf16[12,64,128]{2,1,0:T(8,128)(2,1)S(1)}, u32[]{:S(2)}) copy-start(bf16[12,64,128]{2,1,0:T(8,128)(2,1)S(1)} %convolution_convert_fusion) | copy-start | bytes 589828
  338.2 62.0 %all-to-all-start.1 = ((bf16[128,4,192]{0,2,1:T(8,128)(2,1)}), bf16[128,4,192]{0,2,1:T(8,128)(2,1)}, u32[]{:S(2)}, u32[]{:S(2)}) async-start(bf16[128,4,192]{0,2,1:T(8,128)(2,1)} %bitcast.27), calls=%async_computation.1 | async-start | bytes 393216 | tf_op jit(solution)/shard_map/all_to_all | solution.py:200
  400.2 56.0 %all-to-all-start.3 = ((bf16[128,4,768]{2,0,1:T(8,128)(2,1)}), bf16[128,4,768]{2,0,1:T(8,128)(2,1)S(1)}, u32[]{:S(2)}, u32[]{:S(2)}) async-start(bf16[128,4,768]{2,0,1:T(8,128)(2,1)} %bitcast.115), calls=%async_computation.3 | async-start | bytes 1572864 | tf_op jit(solution)/shard_map/all_to_all | solution.py:202
  406.4 32.5 %copy-start.19 = (bf16[128,768]{1,0:T(8,128)(2,1)S(1)}, bf16[128,768]{1,0:T(8,128)(2,1)}, u32[]{:S(2)}) copy-start(bf16[128,768]{1,0:T(8,128)(2,1)} %copy-done.18) | copy-start | bytes 589828
  456.2 11.6 %all-to-all-start.2 = ((bf16[128,4,192]{0,2,1:T(8,128)(2,1)}), bf16[128,4,192]{0,2,1:T(8,128)(2,1)S(1)}, u32[]{:S(2)}, u32[]{:S(2)}) async-start(bf16[128,4,192]{0,2,1:T(8,128)(2,1)} %bitcast.31), calls=%async_computation.2 | async-start | bytes 393216 | tf_op jit(solution)/shard_map/all_to_all | solution.py:201
  461.5 122.7 %all-reduce.23.cloned.1.call-start = ((), (), s32[]{:S(2)}) async-start(), calls=%async_computation.10 | async-start | bytes 14155776 | tf_op jit(solution)/shard_map/psum | solution.py:247
  471.9 60.2 %copy-start.25 = (f32[128]{0:T(128)S(1)}, f32[128]{0:T(128)}, u32[]{:S(2)}) copy-start(f32[128]{0:T(128)} %copy-done.24) | copy-start | bytes 1540
  471.9 61.7 %copy-start.2 = (bf16[768,768]{1,0:T(8,128)(2,1)S(1)}, bf16[768,768]{1,0:T(8,128)(2,1)}, u32[]{:S(2)}) copy-start(bf16[768,768]{1,0:T(8,128)(2,1)} %all-gather.10.cloned.1.call-done) | copy-start | bytes 3538948
  472.8 62.2 %copy-start.3 = (bf16[768,768]{1,0:T(8,128)(2,1)S(1)}, bf16[768,768]{1,0:T(8,128)(2,1)}, u32[]{:S(2)}) copy-start(bf16[768,768]{1,0:T(8,128)(2,1)} %all-gather.12.cloned.1.call-done) | copy-start | bytes 3538948
  473.5 61.6 %copy-start.17 = (bf16[12,64,128]{2,1,0:T(8,128)(2,1)S(1)}, bf16[12,64,128]{2,1,0:T(8,128)(2,1)}, u32[]{:S(2)}) copy-start(bf16[12,64,128]{2,1,0:T(8,128)(2,1)} %copy-done.16) | copy-start | bytes 589828
  (21 other events, 96.1 us)
Sparse Core Ops, SparseCore 0:
  9.7 60.9 all-gather.9
  72.3 37.6 all-gather.11
  111.6 43.0 all-gather.7
  156.1 30.5 all-gather.13
  188.2 88.6 all-gather.15
  292.3 91.0 all-gather.17
  472.0 112.2 all-reduce.22
